TPU v7x, 128 devices: a whole 4x4x4 slice. The times are simulated.
128 devices in a mesh: probe: 4 (over z_hi, core), sx: 4 (over x), sy: 8 (over y, z_lo).
Axes of the slice: x: 4, y: 4, z: 4 (z_hi: 2, z_lo: 2; z = z_hi * 2 + z_lo), core: 2. Of those that a mesh axis runs over, the one named last changes fastest.
Arguments:
- probes: float32 [8, 128, 256, 256], P('probe', 'sx', 'sy'), may hold values from -6 to 6
- velocity: float32 [3, 128, 256, 256], P(None, 'sx', 'sy'), may hold values from -0.15 to 0.15
- diffusivity: float32 [128, 256, 256], P('sx', 'sy'), may hold values from 0.02 to 0.15
- obs_weight: float32 [128, 256, 256], P('sx', 'sy'), may hold values from 0.05 to 1
Outputs:
- basis_fields: float32 [8, 128, 256, 256], P('probe', 'sx', 'sy')
- projected_hessian: float32 [8, 8], replicated
All inputs are finite; a program needn't handle non-finite values.
Results may differ from a plain program's by a relative error of at most 0.00013.
Values sent between devices are 32-bit elements; how exact they have to be, the bound alone decides.
A program may use at most 128 MiB of HBM per device.

v0:
```python
import jax
import jax.numpy as jnp
from jax import lax
from jax.sharding import PartitionSpec as P

STEPS = 4


def extended(value, sides, width):
    for axis, dim in sides:
        devices, length = (lax.axis_size(axis), value.shape[dim])
        up = [(i, (i + 1) % devices) for i in range(devices - 1)]
        down = [(j, i) for i, j in up]
        last = lax.slice_in_dim(value, length - width, length, axis=dim)
        leading = lax.slice_in_dim(value, 0, width, axis=dim)
        before = lax.ppermute(last, axis, up)
        after = lax.ppermute(leading, axis, down)
        value = jnp.concatenate([before, value, after], axis=dim)
    return value


def forward_step(state, coeffs):
    cc = coeffs[:, 1:-1, 1:-1, :]
    spread = cc[0]
    inner = state[:, 1:-1, 1:-1, :]
    padded = jnp.pad(inner, ((0, 0), (0, 0), (0, 0), (1, 1)))
    result = (1.0 - 6.0 * spread) * inner
    result = (
        result
        + (spread - 0.5 * cc[1]) * state[:, 2:, 1:-1, :]
        + (spread + 0.5 * cc[1]) * state[:, :-2, 1:-1, :]
    )
    result = (
        result
        + (spread - 0.5 * cc[2]) * state[:, 1:-1, 2:, :]
        + (spread + 0.5 * cc[2]) * state[:, 1:-1, :-2, :]
    )
    result = (
        result
        + (spread - 0.5 * cc[3]) * padded[..., 2:]
        + (spread + 0.5 * cc[3]) * padded[..., :-2]
    )
    return result


def adjoint_step(state, coeffs):
    spread = coeffs[0]
    plus_x = (spread - 0.5 * coeffs[1]) * state
    minus_x = (spread + 0.5 * coeffs[1]) * state
    plus_y = (spread - 0.5 * coeffs[2]) * state
    minus_y = (spread + 0.5 * coeffs[2]) * state
    cc = coeffs[:, 1:-1, 1:-1, :]
    inner = state[:, 1:-1, 1:-1, :]
    pad_plus = jnp.pad((cc[0] - 0.5 * cc[3]) * inner, ((0, 0), (0, 0), (0, 0), (1, 1)))
    pad_minus = jnp.pad((cc[0] + 0.5 * cc[3]) * inner, ((0, 0), (0, 0), (0, 0), (1, 1)))
    result = (1.0 - 6.0 * cc[0]) * inner
    result = result + plus_x[:, :-2, 1:-1, :] + minus_x[:, 2:, 1:-1, :]
    result = result + plus_y[:, 1:-1, :-2, :] + minus_y[:, 1:-1, 2:, :]
    result = result + pad_plus[..., :-2] + pad_minus[..., 2:]
    return result


def factor_inverse(gram, count):
    lower = jnp.linalg.cholesky(gram)
    return jax.scipy.linalg.solve_triangular(lower, jnp.eye(count, dtype=jnp.float32), lower=True)


def shards(probes, velocity, diffusivity, obs_weight):
    group = probes.shape[0]
    count = group * lax.axis_size("probe")
    ncells = (
        probes.shape[1]
        * probes.shape[2]
        * probes.shape[3]
        * lax.axis_size("sx")
        * lax.axis_size("sy")
    )
    coeffs = jnp.concatenate([diffusivity[None], velocity], axis=0)
    highest = lax.Precision.HIGHEST
    edge_coeffs = extended(coeffs, (("sx", 1), ("sy", 2)), 1)

    def forward(state):
        for step in range(STEPS):
            padded = extended(state, (("sx", 1), ("sy", 2)), 1)
            state = forward_step(padded, edge_coeffs)
        return state

    state = obs_weight * forward(probes)
    for step in range(STEPS):
        padded = extended(state, (("sx", 1), ("sy", 2)), 1)
        state = adjoint_step(padded, edge_coeffs)
    images = state
    again = forward(images)
    root = jnp.sqrt(obs_weight) * again
    both = jnp.stack([images, root], axis=1)
    slabs = lax.all_to_all(both, "probe", split_axis=2, concat_axis=0, tiled=True)
    flat = slabs[:, 0].reshape(count, -1)
    flat_root = slabs[:, 1].reshape(count, -1)
    partial_gram = jnp.dot(flat, flat.T, precision=highest)
    partial_cross = jnp.dot(flat_root, flat_root.T, precision=highest)
    sums = lax.psum(jnp.stack([partial_gram, partial_cross]), ("probe", "sx", "sy")) / ncells
    gram, cross = (sums[0], sums[1])
    inverse = factor_inverse(gram, count)
    basis_slab = jnp.dot(inverse, flat, precision=highest)
    basis_fields = lax.all_to_all(
        basis_slab.reshape(slabs[:, 0].shape), "probe", split_axis=0, concat_axis=1, tiled=True
    )
    projected = jnp.dot(jnp.dot(inverse, cross, precision=highest), inverse.T, precision=highest)
    return (basis_fields, projected)


def solution(mesh):
    return jax.shard_map(
        shards,
        mesh=mesh,
        in_specs=(
            P("probe", "sx", "sy", None),
            P(None, "sx", "sy", None),
            P("sx", "sy", None),
            P("sx", "sy", None),
        ),
        out_specs=(P("probe", "sx", "sy", None), P()),
        check_vma=False,
    )
```

profile of v0, /device:TPU:1, one launch (start us, length us, event | category | flops | bytes accessed | tf_op | source)
XLA Modules:
  0.0 471.6 jit_solution(13638757533432052887)
XLA Ops:
  3.0 4.6 collective-permute-start.1
  12.0 4.4 collective-permute-start.3
  21.8 3.5 fusion.10
  26.7 4.0 collective-permute-start.5
  33.3 4.9 %collective-permute-start.7 = (f32[2,34,1,256]{3,1,2,0:T(8,128)S(1)}, f32[2,34,1,256]{3,1,2,0:T(8,128)S(1)}, u32[]{:S(2)}, u32[]{:S(2)}) collective-permute-start(f32[2,34,1,256]{3,1,2,0:T(8,128)S(1)} %get-tuple-element.46), channel_id=1, source_target_pairs={{0,1},{1,2},{2,3},{3,4},{4,5},{5,6},{6,7},{8,9},{9,10},{10,11},{11... | collective-permute-start | bytes 208904 | tf_op jit(solution)/shard_map/ppermute | solution.py:16
  38.3 4.0 collective-permute-start.16
  43.6 3.5 fusion.14
  48.4 4.6 collective-permute-start.9
  53.3 4.4 collective-permute-start.18
  60.4 4.8 %collective-permute-start.11 = (f32[2,34,1,256]{3,1,2,0:T(8,128)S(1)}, f32[2,34,1,256]{3,1,2,0:T(8,128)S(1)}, u32[]{:S(2)}, u32[]{:S(2)}) collective-permute-start(f32[2,34,1,256]{3,1,2,0:T(8,128)S(1)} %get-tuple-element.44), channel_id=1, source_target_pairs={{0,1},{1,2},{2,3},{3,4},{4,5},{5,6},{6,7},{8,9},{9,10},{10,11},{11... | collective-permute-start | bytes 208904 | tf_op jit(solution)/shard_map/ppermute | solution.py:16
  68.3 3.4 fusion.18
  73.1 4.3 collective-permute-start.13
  80.0 4.4 collective-permute-start.15
  85.9 3.5 broadcast_multiply_fusion.3
  89.6 3.7 collective-permute-start.20
  98.3 4.3 collective-permute-start.22
  105.5 3.5 collective-permute-done.23
  109.5 3.9 broadcast_multiply_fusion.2
  113.5 3.5 collective-permute-start.24
  118.4 3.7 collective-permute-done.25
  122.1 4.3 collective-permute-start.26
  132.0 3.9 broadcast_multiply_fusion.1
  140.7 3.9 collective-permute-done.29
  149.4 3.5 collective-permute-done.31
  153.3 3.7 broadcast_multiply_fusion
  161.4 3.7 collective-permute-done.33
  165.1 4.3 collective-permute-start.34
  171.1 3.4 collective-permute-done.35
  179.1 4.0 collective-permute-start.37
  185.8 4.0 collective-permute-start.39
  192.0 3.4 fusion.27
  196.8 4.0 collective-permute-start.41
  203.5 4.4 collective-permute-start.43
  210.5 3.4 fusion.31
  215.3 4.4 collective-permute-start.45
  222.4 4.4 collective-permute-start.47
  233.2 4.6 collective-permute-start.49
  240.4 5.3 %collective-permute-start.51 = (f32[2,34,1,256]{3,1,2,0:T(8,128)S(1)}, f32[2,34,1,256]{3,1,2,0:T(8,128)S(1)}, u32[]{:S(2)}, u32[]{:S(2)}) collective-permute-start(f32[2,34,1,256]{3,1,2,0:T(8,128)S(1)} %get-tuple-element.26), channel_id=1, source_target_pairs={{0,1},{1,2},{2,3},{3,4},{4,5},{5,6},{6,7},{8,9},{9,10},{10,11},{11... | collective-permute-start | bytes 208904 | tf_op jit(solution)/shard_map/ppermute | solution.py:16
  247.1 3.5 fusion.41
  253.3 79.6 %all_to_all.36 = f32[2,2,32,32,256]{4,3,0,1,2:T(8,128)S(1)} all-to-all(f32[2,2,32,32,256]{4,3,0,1,2:T(8,128)S(1)} %copy.58), channel_id=1, replica_groups=mesh['probe'=4,'sx'=4,'sy'=8] {'probe'}, dimensions={2} | all-to-all | bytes 8388608 | tf_op jit(solution)/shard_map/all_to_all | solution.py:96
  333.0 5.2 %copy.72 = f32[2,2,4,8,32,256]{5,0,2,4,3,1:T(2,128)} copy(f32[2,2,4,8,32,256]{5,4,0,1,3,2:T(8,128)S(1)} %bitcast.90) | data formatting | bytes 8388608 | tf_op jit(solution)/shard_map/all_to_all | solution.py:96
  338.2 6.1 %all_to_all.29 = f32[8,2,8,32,256]{4,0,3,2,1:T(8,128)} reshape(f32[4,2,2,8,32,256]{5,1,0,4,3,2:T(2,128)} %bitcast.91) | data formatting | bytes 8388608 | tf_op jit(solution)/shard_map/all_to_all | solution.py:96
  344.4 7.1 %fusion.131 = f32[1,8,8]{2,1,0:T(8,128)S(1)} fusion(f32[8,2,8,32,256]{4,0,3,2,1:T(8,128)} %all_to_all.29), kind=kOutput, calls=%fused_computation.253 | convolution fusion | flops 50331648 | bytes 2097408 | tf_op jit(solution)/shard_map/dot_general | solution.py:99
  351.5 7.1 %fusion.134 = f32[1,8,8]{2,1,0:T(8,128)S(1)} fusion(f32[8,2,8,32,256]{4,0,3,2,1:T(8,128)} %all_to_all.29), kind=kOutput, calls=%fused_computation.254 | convolution fusion | flops 50331648 | bytes 2097408 | tf_op jit(solution)/shard_map/dot_general | solution.py:100
  358.6 72.6 %psum.7 = f32[2,8,8]{2,1,0:T(8,128)S(1)} all-reduce(f32[2,8,8]{2,1,0:T(8,128)S(1)} %pad_maximum_fusion.117), channel_id=1, replica_groups=mesh['probe'=4,'sx'=4,'sy'=8] {'probe','sx','sy'}, use_global_device_ids=true, to_apply=%region_0.1 | all-reduce | flops 128 | bytes 1024 | tf_op jit(solution)/shard_map/psum | solution.py:101
  434.2 3.4 fusion.124
  439.6 4.1 all-to-all-start.1
  444.6 25.3 %all-to-all-done.1 = f32[8,8,32,256]{3,2,1,0:T(8,128)S(1)} async-done(((f32[8,8,32,256]{3,2,1,0:T(8,128)}), f32[8,8,32,256]{3,2,1,0:T(8,128)S(1)}, u32[]{:S(2)}, u32[]{:S(2)}) %all-to-all-start.1) | async-done | bytes 2097184 | tf_op jit(solution)/shard_map/all_to_all | solution.py:105
  (167 shorter events, 101.8 us)
Async XLA Ops:
  1.6 8.9 %collective-permute-start = (f32[2,1,32,256]{3,1,2,0:T(1,128)S(1)}, f32[2,1,32,256]{3,1,2,0:T(1,128)S(1)}, u32[]{:S(2)}, u32[]{:S(2)}) collective-permute-start(f32[2,1,32,256]{3,1,2,0:T(1,128)S(1)} %copy.38), channel_id=1, source_target_pairs={{8,0},{16,8},{24,16},{9,1},{17,9},{25,17},{10,2},{18,10},{26,18},{... | collective-permute-start | bytes 196616 | tf_op jit(solution)/shard_map/ppermute | solution.py:17
  3.0 7.6 %collective-permute-start.1 = (f32[2,1,32,256]{3,1,2,0:T(1,128)S(1)}, f32[2,1,32,256]{3,1,2,0:T(1,128)S(1)}, u32[]{:S(2)}, u32[]{:S(2)}) collective-permute-start(f32[2,1,32,256]{3,1,2,0:T(1,128)S(1)} %copy.41), channel_id=1, source_target_pairs={{0,8},{8,16},{16,24},{1,9},{9,17},{17,25},{2,10},{10,18},{18,26},{... | collective-permute-start | bytes 196616 | tf_op jit(solution)/shard_map/ppermute | solution.py:16
  10.6 11.2 %collective-permute-start.2 = (f32[2,34,1,256]{3,1,2,0:T(8,128)S(1)}, f32[2,34,1,256]{3,1,2,0:T(8,128)S(1)}, u32[]{:S(2)}, u32[]{:S(2)}) collective-permute-start(f32[2,34,1,256]{3,1,2,0:T(8,128)S(1)} %get-tuple-element.47), channel_id=1, source_target_pairs={{1,0},{2,1},{3,2},{4,3},{5,4},{6,5},{7,6},{9,8},{10,9},{11,10},{12... | collective-permute-start | bytes 208904 | tf_op jit(solution)/shard_map/ppermute | solution.py:17
  12.0 9.8 %collective-permute-start.3 = (f32[2,34,1,256]{3,1,2,0:T(8,128)S(1)}, f32[2,34,1,256]{3,1,2,0:T(8,128)S(1)}, u32[]{:S(2)}, u32[]{:S(2)}) collective-permute-start(f32[2,34,1,256]{3,1,2,0:T(8,128)S(1)} %get-tuple-element.48), channel_id=1, source_target_pairs={{0,1},{1,2},{2,3},{3,4},{4,5},{5,6},{6,7},{8,9},{9,10},{10,11},{11... | collective-permute-start | bytes 208904 | tf_op jit(solution)/shard_map/ppermute | solution.py:16
  25.4 5.3 %collective-permute-start.4 = (f32[2,1,32,256]{3,1,2,0:T(1,128)S(1)}, f32[2,1,32,256]{3,1,2,0:T(1,128)S(1)}, u32[]{:S(2)}, u32[]{:S(2)}) collective-permute-start(f32[2,1,32,256]{3,1,2,0:T(1,128)S(1)} %get-tuple-element.70), channel_id=1, source_target_pairs={{8,0},{16,8},{24,16},{9,1},{17,9},{25,17},{10,2},{18,10},{26,18},{... | collective-permute-start | bytes 196616 | tf_op jit(solution)/shard_map/ppermute | solution.py:17
  26.7 5.3 %collective-permute-start.5 = (f32[2,1,32,256]{3,1,2,0:T(1,128)S(1)}, f32[2,1,32,256]{3,1,2,0:T(1,128)S(1)}, u32[]{:S(2)}, u32[]{:S(2)}) collective-permute-start(f32[2,1,32,256]{3,1,2,0:T(1,128)S(1)} %get-tuple-element.69), channel_id=1, source_target_pairs={{0,8},{8,16},{16,24},{1,9},{9,17},{17,25},{2,10},{10,18},{18,26},{... | collective-permute-start | bytes 196616 | tf_op jit(solution)/shard_map/ppermute | solution.py:16
  32.0 11.5 %collective-permute-start.6 = (f32[2,34,1,256]{3,1,2,0:T(8,128)S(1)}, f32[2,34,1,256]{3,1,2,0:T(8,128)S(1)}, u32[]{:S(2)}, u32[]{:S(2)}) collective-permute-start(f32[2,34,1,256]{3,1,2,0:T(8,128)S(1)} %get-tuple-element.45), channel_id=1, source_target_pairs={{1,0},{2,1},{3,2},{4,3},{5,4},{6,5},{7,6},{9,8},{10,9},{11,10},{12... | collective-permute-start | bytes 208904 | tf_op jit(solution)/shard_map/ppermute | solution.py:17
  33.3 10.2 %collective-permute-start.7 = (f32[2,34,1,256]{3,1,2,0:T(8,128)S(1)}, f32[2,34,1,256]{3,1,2,0:T(8,128)S(1)}, u32[]{:S(2)}, u32[]{:S(2)}) collective-permute-start(f32[2,34,1,256]{3,1,2,0:T(8,128)S(1)} %get-tuple-element.46), channel_id=1, source_target_pairs={{0,1},{1,2},{2,3},{3,4},{4,5},{5,6},{6,7},{8,9},{9,10},{10,11},{11... | collective-permute-start | bytes 208904 | tf_op jit(solution)/shard_map/ppermute | solution.py:16
  38.3 14.8 %collective-permute-start.16 = (f32[4,1,32,256]{3,2,1,0:T(8,128)S(1)}, f32[4,1,32,256]{3,2,1,0:T(8,128)S(1)}, u32[]{:S(2)}, u32[]{:S(2)}) collective-permute-start(f32[4,1,32,256]{3,2,1,0:T(8,128)S(1)} %get-tuple-element.17), channel_id=1, source_target_pairs={{0,8},{8,16},{16,24},{1,9},{9,17},{17,25},{2,10},{10,18},{18,26},{... | collective-permute-start | bytes 393224 | tf_op jit(solution)/shard_map/ppermute | solution.py:16
  42.3 10.8 %collective-permute-start.17 = (f32[4,1,32,256]{3,2,1,0:T(8,128)S(1)}, f32[4,1,32,256]{3,2,1,0:T(8,128)S(1)}, u32[]{:S(2)}, u32[]{:S(2)}) collective-permute-start(f32[4,1,32,256]{3,2,1,0:T(8,128)S(1)} %get-tuple-element.18), channel_id=1, source_target_pairs={{8,0},{16,8},{24,16},{9,1},{17,9},{25,17},{10,2},{18,10},{26,18},{... | collective-permute-start | bytes 393224 | tf_op jit(solution)/shard_map/ppermute | solution.py:17
  47.1 11.9 %collective-permute-start.8 = (f32[2,1,32,256]{3,1,2,0:T(1,128)S(1)}, f32[2,1,32,256]{3,1,2,0:T(1,128)S(1)}, u32[]{:S(2)}, u32[]{:S(2)}) collective-permute-start(f32[2,1,32,256]{3,1,2,0:T(1,128)S(1)} %get-tuple-element.68), channel_id=1, source_target_pairs={{8,0},{16,8},{24,16},{9,1},{17,9},{25,17},{10,2},{18,10},{26,18},{... | collective-permute-start | bytes 196616 | tf_op jit(solution)/shard_map/ppermute | solution.py:17
  48.4 10.6 %collective-permute-start.9 = (f32[2,1,32,256]{3,1,2,0:T(1,128)S(1)}, f32[2,1,32,256]{3,1,2,0:T(1,128)S(1)}, u32[]{:S(2)}, u32[]{:S(2)}) collective-permute-start(f32[2,1,32,256]{3,1,2,0:T(1,128)S(1)} %get-tuple-element.67), channel_id=1, source_target_pairs={{0,8},{8,16},{16,24},{1,9},{9,17},{17,25},{2,10},{10,18},{18,26},{... | collective-permute-start | bytes 196616 | tf_op jit(solution)/shard_map/ppermute | solution.py:16
  53.3 12.5 %collective-permute-start.18 = (f32[4,34,1,256]{3,1,2,0:T(8,128)S(1)}, f32[4,34,1,256]{3,1,2,0:T(8,128)S(1)}, u32[]{:S(2)}, u32[]{:S(2)}) collective-permute-start(f32[4,34,1,256]{3,1,2,0:T(8,128)S(1)} %copy.49), channel_id=1, source_target_pairs={{0,1},{1,2},{2,3},{3,4},{4,5},{5,6},{6,7},{8,9},{9,10},{10,11},{11... | collective-permute-start | bytes 417800 | tf_op jit(solution)/shard_map/ppermute | solution.py:16
  57.8 8.2 %collective-permute-start.19 = (f32[4,34,1,256]{3,1,2,0:T(8,128)S(1)}, f32[4,34,1,256]{3,1,2,0:T(8,128)S(1)}, u32[]{:S(2)}, u32[]{:S(2)}) collective-permute-start(f32[4,34,1,256]{3,1,2,0:T(8,128)S(1)} %copy.50), channel_id=1, source_target_pairs={{1,0},{2,1},{3,2},{4,3},{5,4},{6,5},{7,6},{9,8},{10,9},{11,10},{12... | collective-permute-start | bytes 417800 | tf_op jit(solution)/shard_map/ppermute | solution.py:17
  59.1 7.1 %collective-permute-start.10 = (f32[2,34,1,256]{3,1,2,0:T(8,128)S(1)}, f32[2,34,1,256]{3,1,2,0:T(8,128)S(1)}, u32[]{:S(2)}, u32[]{:S(2)}) collective-permute-start(f32[2,34,1,256]{3,1,2,0:T(8,128)S(1)} %get-tuple-element.43), channel_id=1, source_target_pairs={{1,0},{2,1},{3,2},{4,3},{5,4},{6,5},{7,6},{9,8},{10,9},{11,10},{12... | collective-permute-start | bytes 208904 | tf_op jit(solution)/shard_map/ppermute | solution.py:17
  60.4 7.9 %collective-permute-start.11 = (f32[2,34,1,256]{3,1,2,0:T(8,128)S(1)}, f32[2,34,1,256]{3,1,2,0:T(8,128)S(1)}, u32[]{:S(2)}, u32[]{:S(2)}) collective-permute-start(f32[2,34,1,256]{3,1,2,0:T(8,128)S(1)} %get-tuple-element.44), channel_id=1, source_target_pairs={{0,1},{1,2},{2,3},{3,4},{4,5},{5,6},{6,7},{8,9},{9,10},{10,11},{11... | collective-permute-start | bytes 208904 | tf_op jit(solution)/shard_map/ppermute | solution.py:16
  71.8 6.1 %collective-permute-start.12 = (f32[2,1,32,256]{3,1,2,0:T(1,128)S(1)}, f32[2,1,32,256]{3,1,2,0:T(1,128)S(1)}, u32[]{:S(2)}, u32[]{:S(2)}) collective-permute-start(f32[2,1,32,256]{3,1,2,0:T(1,128)S(1)} %get-tuple-element.66), channel_id=1, source_target_pairs={{8,0},{16,8},{24,16},{9,1},{17,9},{25,17},{10,2},{18,10},{26,18},{... | collective-permute-start | bytes 196616 | tf_op jit(solution)/shard_map/ppermute | solution.py:17
  73.1 5.6 %collective-permute-start.13 = (f32[2,1,32,256]{3,1,2,0:T(1,128)S(1)}, f32[2,1,32,256]{3,1,2,0:T(1,128)S(1)}, u32[]{:S(2)}, u32[]{:S(2)}) collective-permute-start(f32[2,1,32,256]{3,1,2,0:T(1,128)S(1)} %get-tuple-element.65), channel_id=1, source_target_pairs={{0,8},{8,16},{16,24},{1,9},{9,17},{17,25},{2,10},{10,18},{18,26},{... | collective-permute-start | bytes 196616 | tf_op jit(solution)/shard_map/ppermute | solution.py:16
  78.7 6.1 %collective-permute-start.14 = (f32[2,34,1,256]{3,1,2,0:T(8,128)S(1)}, f32[2,34,1,256]{3,1,2,0:T(8,128)S(1)}, u32[]{:S(2)}, u32[]{:S(2)}) collective-permute-start(f32[2,34,1,256]{3,1,2,0:T(8,128)S(1)} %get-tuple-element.41), channel_id=1, source_target_pairs={{1,0},{2,1},{3,2},{4,3},{5,4},{6,5},{7,6},{9,8},{10,9},{11,10},{12... | collective-permute-start | bytes 208904 | tf_op jit(solution)/shard_map/ppermute | solution.py:17
  80.0 5.9 %collective-permute-start.15 = (f32[2,34,1,256]{3,1,2,0:T(8,128)S(1)}, f32[2,34,1,256]{3,1,2,0:T(8,128)S(1)}, u32[]{:S(2)}, u32[]{:S(2)}) collective-permute-start(f32[2,34,1,256]{3,1,2,0:T(8,128)S(1)} %get-tuple-element.42), channel_id=1, source_target_pairs={{0,1},{1,2},{2,3},{3,4},{4,5},{5,6},{6,7},{8,9},{9,10},{10,11},{11... | collective-permute-start | bytes 208904 | tf_op jit(solution)/shard_map/ppermute | solution.py:16
  89.6 8.2 %collective-permute-start.20 = (f32[2,1,32,256]{3,1,2,0:T(1,128)S(1)}, f32[2,1,32,256]{3,1,2,0:T(1,128)S(1)}, u32[]{:S(2)}, u32[]{:S(2)}) collective-permute-start(f32[2,1,32,256]{3,1,2,0:T(1,128)S(1)} %get-tuple-element.63), channel_id=1, source_target_pairs={{0,8},{8,16},{16,24},{1,9},{9,17},{17,25},{2,10},{10,18},{18,26},{... | collective-permute-start | bytes 196616 | tf_op jit(solution)/shard_map/ppermute | solution.py:16
  93.3 5.0 %collective-permute-start.21 = (f32[2,1,32,256]{3,1,2,0:T(1,128)S(1)}, f32[2,1,32,256]{3,1,2,0:T(1,128)S(1)}, u32[]{:S(2)}, u32[]{:S(2)}) collective-permute-start(f32[2,1,32,256]{3,1,2,0:T(1,128)S(1)} %get-tuple-element.64), channel_id=1, source_target_pairs={{8,0},{16,8},{24,16},{9,1},{17,9},{25,17},{10,2},{18,10},{26,18},{... | collective-permute-start | bytes 196616 | tf_op jit(solution)/shard_map/ppermute | solution.py:17
  98.3 7.2 %collective-permute-start.22 = (f32[2,34,1,256]{3,1,2,0:T(8,128)S(1)}, f32[2,34,1,256]{3,1,2,0:T(8,128)S(1)}, u32[]{:S(2)}, u32[]{:S(2)}) collective-permute-start(f32[2,34,1,256]{3,1,2,0:T(8,128)S(1)} %get-tuple-element.39), channel_id=1, source_target_pairs={{0,1},{1,2},{2,3},{3,4},{4,5},{5,6},{6,7},{8,9},{9,10},{10,11},{11... | collective-permute-start | bytes 208904 | tf_op jit(solution)/shard_map/ppermute | solution.py:16
  102.6 6.4 %collective-permute-start.23 = (f32[2,34,1,256]{3,1,2,0:T(8,128)S(1)}, f32[2,34,1,256]{3,1,2,0:T(8,128)S(1)}, u32[]{:S(2)}, u32[]{:S(2)}) collective-permute-start(f32[2,34,1,256]{3,1,2,0:T(8,128)S(1)} %get-tuple-element.40), channel_id=1, source_target_pairs={{1,0},{2,1},{3,2},{4,3},{5,4},{6,5},{7,6},{9,8},{10,9},{11,10},{12... | collective-permute-start | bytes 208904 | tf_op jit(solution)/shard_map/ppermute | solution.py:17
  117.0 5.0 %collective-permute-start.25 = (f32[2,1,32,256]{3,1,2,0:T(1,128)S(1)}, f32[2,1,32,256]{3,1,2,0:T(1,128)S(1)}, u32[]{:S(2)}, u32[]{:S(2)}) collective-permute-start(f32[2,1,32,256]{3,1,2,0:T(1,128)S(1)} %get-tuple-element.62), channel_id=1, source_target_pairs={{8,0},{16,8},{24,16},{9,1},{17,9},{25,17},{10,2},{18,10},{26,18},{... | collective-permute-start | bytes 196616 | tf_op jit(solution)/shard_map/ppermute | solution.py:17
  122.1 7.6 %collective-permute-start.26 = (f32[2,34,1,256]{3,1,2,0:T(8,128)S(1)}, f32[2,34,1,256]{3,1,2,0:T(8,128)S(1)}, u32[]{:S(2)}, u32[]{:S(2)}) collective-permute-start(f32[2,34,1,256]{3,1,2,0:T(8,128)S(1)} %get-tuple-element.37), channel_id=1, source_target_pairs={{0,1},{1,2},{2,3},{3,4},{4,5},{5,6},{6,7},{8,9},{9,10},{10,11},{11... | collective-permute-start | bytes 208904 | tf_op jit(solution)/shard_map/ppermute | solution.py:16
  126.3 5.2 %collective-permute-start.27 = (f32[2,34,1,256]{3,1,2,0:T(8,128)S(1)}, f32[2,34,1,256]{3,1,2,0:T(8,128)S(1)}, u32[]{:S(2)}, u32[]{:S(2)}) collective-permute-start(f32[2,34,1,256]{3,1,2,0:T(8,128)S(1)} %get-tuple-element.38), channel_id=1, source_target_pairs={{1,0},{2,1},{3,2},{4,3},{5,4},{6,5},{7,6},{9,8},{10,9},{11,10},{12... | collective-permute-start | bytes 208904 | tf_op jit(solution)/shard_map/ppermute | solution.py:17
  139.4 5.2 %collective-permute-start.29 = (f32[2,1,32,256]{3,1,2,0:T(1,128)S(1)}, f32[2,1,32,256]{3,1,2,0:T(1,128)S(1)}, u32[]{:S(2)}, u32[]{:S(2)}) collective-permute-start(f32[2,1,32,256]{3,1,2,0:T(1,128)S(1)} %get-tuple-element.60), channel_id=1, source_target_pairs={{8,0},{16,8},{24,16},{9,1},{17,9},{25,17},{10,2},{18,10},{26,18},{... | collective-permute-start | bytes 196616 | tf_op jit(solution)/shard_map/ppermute | solution.py:17
  147.7 5.2 %collective-permute-start.31 = (f32[2,34,1,256]{3,1,2,0:T(8,128)S(1)}, f32[2,34,1,256]{3,1,2,0:T(8,128)S(1)}, u32[]{:S(2)}, u32[]{:S(2)}) collective-permute-start(f32[2,34,1,256]{3,1,2,0:T(8,128)S(1)} %get-tuple-element.36), channel_id=1, source_target_pairs={{1,0},{2,1},{3,2},{4,3},{5,4},{6,5},{7,6},{9,8},{10,9},{11,10},{12... | collective-permute-start | bytes 208904 | tf_op jit(solution)/shard_map/ppermute | solution.py:17
  165.1 6.0 %collective-permute-start.34 = (f32[2,34,1,256]{3,1,2,0:T(8,128)S(1)}, f32[2,34,1,256]{3,1,2,0:T(8,128)S(1)}, u32[]{:S(2)}, u32[]{:S(2)}) collective-permute-start(f32[2,34,1,256]{3,1,2,0:T(8,128)S(1)} %get-tuple-element.33), channel_id=1, source_target_pairs={{0,1},{1,2},{2,3},{3,4},{4,5},{5,6},{6,7},{8,9},{9,10},{10,11},{11... | collective-permute-start | bytes 208904 | tf_op jit(solution)/shard_map/ppermute | solution.py:16
  169.4 5.2 %collective-permute-start.35 = (f32[2,34,1,256]{3,1,2,0:T(8,128)S(1)}, f32[2,34,1,256]{3,1,2,0:T(8,128)S(1)}, u32[]{:S(2)}, u32[]{:S(2)}) collective-permute-start(f32[2,34,1,256]{3,1,2,0:T(8,128)S(1)} %get-tuple-element.34), channel_id=1, source_target_pairs={{1,0},{2,1},{3,2},{4,3},{5,4},{6,5},{7,6},{9,8},{10,9},{11,10},{12... | collective-permute-start | bytes 208904 | tf_op jit(solution)/shard_map/ppermute | solution.py:17
  177.8 5.3 %collective-permute-start.36 = (f32[2,1,32,256]{3,1,2,0:T(1,128)S(1)}, f32[2,1,32,256]{3,1,2,0:T(1,128)S(1)}, u32[]{:S(2)}, u32[]{:S(2)}) collective-permute-start(f32[2,1,32,256]{3,1,2,0:T(1,128)S(1)} %get-tuple-element.56), channel_id=1, source_target_pairs={{8,0},{16,8},{24,16},{9,1},{17,9},{25,17},{10,2},{18,10},{26,18},{... | collective-permute-start | bytes 196616 | tf_op jit(solution)/shard_map/ppermute | solution.py:17
  179.1 5.3 %collective-permute-start.37 = (f32[2,1,32,256]{3,1,2,0:T(1,128)S(1)}, f32[2,1,32,256]{3,1,2,0:T(1,128)S(1)}, u32[]{:S(2)}, u32[]{:S(2)}) collective-permute-start(f32[2,1,32,256]{3,1,2,0:T(1,128)S(1)} %get-tuple-element.55), channel_id=1, source_target_pairs={{0,8},{8,16},{16,24},{1,9},{9,17},{17,25},{2,10},{10,18},{18,26},{... | collective-permute-start | bytes 196616 | tf_op jit(solution)/shard_map/ppermute | solution.py:16
  184.5 5.3 %collective-permute-start.38 = (f32[2,34,1,256]{3,1,2,0:T(8,128)S(1)}, f32[2,34,1,256]{3,1,2,0:T(8,128)S(1)}, u32[]{:S(2)}, u32[]{:S(2)}) collective-permute-start(f32[2,34,1,256]{3,1,2,0:T(8,128)S(1)} %get-tuple-element.31), channel_id=1, source_target_pairs={{1,0},{2,1},{3,2},{4,3},{5,4},{6,5},{7,6},{9,8},{10,9},{11,10},{12... | collective-permute-start | bytes 208904 | tf_op jit(solution)/shard_map/ppermute | solution.py:17
  185.8 6.2 %collective-permute-start.39 = (f32[2,34,1,256]{3,1,2,0:T(8,128)S(1)}, f32[2,34,1,256]{3,1,2,0:T(8,128)S(1)}, u32[]{:S(2)}, u32[]{:S(2)}) collective-permute-start(f32[2,34,1,256]{3,1,2,0:T(8,128)S(1)} %get-tuple-element.32), channel_id=1, source_target_pairs={{0,1},{1,2},{2,3},{3,4},{4,5},{5,6},{6,7},{8,9},{9,10},{10,11},{11... | collective-permute-start | bytes 208904 | tf_op jit(solution)/shard_map/ppermute | solution.py:16
  195.5 5.3 %collective-permute-start.40 = (f32[2,1,32,256]{3,1,2,0:T(1,128)S(1)}, f32[2,1,32,256]{3,1,2,0:T(1,128)S(1)}, u32[]{:S(2)}, u32[]{:S(2)}) collective-permute-start(f32[2,1,32,256]{3,1,2,0:T(1,128)S(1)} %get-tuple-element.54), channel_id=1, source_target_pairs={{8,0},{16,8},{24,16},{9,1},{17,9},{25,17},{10,2},{18,10},{26,18},{... | collective-permute-start | bytes 196616 | tf_op jit(solution)/shard_map/ppermute | solution.py:17
  196.8 5.3 %collective-permute-start.41 = (f32[2,1,32,256]{3,1,2,0:T(1,128)S(1)}, f32[2,1,32,256]{3,1,2,0:T(1,128)S(1)}, u32[]{:S(2)}, u32[]{:S(2)}) collective-permute-start(f32[2,1,32,256]{3,1,2,0:T(1,128)S(1)} %get-tuple-element.53), channel_id=1, source_target_pairs={{0,8},{8,16},{16,24},{1,9},{9,17},{17,25},{2,10},{10,18},{18,26},{... | collective-permute-start | bytes 196616 | tf_op jit(solution)/shard_map/ppermute | solution.py:16
  202.2 5.8 %collective-permute-start.42 = (f32[2,34,1,256]{3,1,2,0:T(8,128)S(1)}, f32[2,34,1,256]{3,1,2,0:T(8,128)S(1)}, u32[]{:S(2)}, u32[]{:S(2)}) collective-permute-start(f32[2,34,1,256]{3,1,2,0:T(8,128)S(1)} %get-tuple-element.29), channel_id=1, source_target_pairs={{1,0},{2,1},{3,2},{4,3},{5,4},{6,5},{7,6},{9,8},{10,9},{11,10},{12... | collective-permute-start | bytes 208904 | tf_op jit(solution)/shard_map/ppermute | solution.py:17
  203.5 7.0 %collective-permute-start.43 = (f32[2,34,1,256]{3,1,2,0:T(8,128)S(1)}, f32[2,34,1,256]{3,1,2,0:T(8,128)S(1)}, u32[]{:S(2)}, u32[]{:S(2)}) collective-permute-start(f32[2,34,1,256]{3,1,2,0:T(8,128)S(1)} %get-tuple-element.30), channel_id=1, source_target_pairs={{0,1},{1,2},{2,3},{3,4},{4,5},{5,6},{6,7},{8,9},{9,10},{10,11},{11... | collective-permute-start | bytes 208904 | tf_op jit(solution)/shard_map/ppermute | solution.py:16
  214.0 5.8 %collective-permute-start.44 = (f32[2,1,32,256]{3,1,2,0:T(1,128)S(1)}, f32[2,1,32,256]{3,1,2,0:T(1,128)S(1)}, u32[]{:S(2)}, u32[]{:S(2)}) collective-permute-start(f32[2,1,32,256]{3,1,2,0:T(1,128)S(1)} %get-tuple-element.52), channel_id=1, source_target_pairs={{8,0},{16,8},{24,16},{9,1},{17,9},{25,17},{10,2},{18,10},{26,18},{... | collective-permute-start | bytes 196616 | tf_op jit(solution)/shard_map/ppermute | solution.py:17
  215.3 5.8 %collective-permute-start.45 = (f32[2,1,32,256]{3,1,2,0:T(1,128)S(1)}, f32[2,1,32,256]{3,1,2,0:T(1,128)S(1)}, u32[]{:S(2)}, u32[]{:S(2)}) collective-permute-start(f32[2,1,32,256]{3,1,2,0:T(1,128)S(1)} %get-tuple-element.51), channel_id=1, source_target_pairs={{0,8},{8,16},{16,24},{1,9},{9,17},{17,25},{2,10},{10,18},{18,26},{... | collective-permute-start | bytes 196616 | tf_op jit(solution)/shard_map/ppermute | solution.py:16
  221.1 5.8 %collective-permute-start.46 = (f32[2,34,1,256]{3,1,2,0:T(8,128)S(1)}, f32[2,34,1,256]{3,1,2,0:T(8,128)S(1)}, u32[]{:S(2)}, u32[]{:S(2)}) collective-permute-start(f32[2,34,1,256]{3,1,2,0:T(8,128)S(1)} %get-tuple-element.27), channel_id=1, source_target_pairs={{1,0},{2,1},{3,2},{4,3},{5,4},{6,5},{7,6},{9,8},{10,9},{11,10},{12... | collective-permute-start | bytes 208904 | tf_op jit(solution)/shard_map/ppermute | solution.py:17
  222.4 5.9 %collective-permute-start.47 = (f32[2,34,1,256]{3,1,2,0:T(8,128)S(1)}, f32[2,34,1,256]{3,1,2,0:T(8,128)S(1)}, u32[]{:S(2)}, u32[]{:S(2)}) collective-permute-start(f32[2,34,1,256]{3,1,2,0:T(8,128)S(1)} %get-tuple-element.28), channel_id=1, source_target_pairs={{0,1},{1,2},{2,3},{3,4},{4,5},{5,6},{6,7},{8,9},{9,10},{10,11},{11... | collective-permute-start | bytes 208904 | tf_op jit(solution)/shard_map/ppermute | solution.py:16
  231.7 6.1 %collective-permute-start.48 = (f32[2,1,32,256]{3,1,2,0:T(1,128)S(1)}, f32[2,1,32,256]{3,1,2,0:T(1,128)S(1)}, u32[]{:S(2)}, u32[]{:S(2)}) collective-permute-start(f32[2,1,32,256]{3,1,2,0:T(1,128)S(1)} %get-tuple-element.50), channel_id=1, source_target_pairs={{8,0},{16,8},{24,16},{9,1},{17,9},{25,17},{10,2},{18,10},{26,18},{... | collective-permute-start | bytes 196616 | tf_op jit(solution)/shard_map/ppermute | solution.py:17
  233.2 5.9 %collective-permute-start.49 = (f32[2,1,32,256]{3,1,2,0:T(1,128)S(1)}, f32[2,1,32,256]{3,1,2,0:T(1,128)S(1)}, u32[]{:S(2)}, u32[]{:S(2)}) collective-permute-start(f32[2,1,32,256]{3,1,2,0:T(1,128)S(1)} %get-tuple-element.49), channel_id=1, source_target_pairs={{0,8},{8,16},{16,24},{1,9},{9,17},{17,25},{2,10},{10,18},{18,26},{... | collective-permute-start | bytes 196616 | tf_op jit(solution)/shard_map/ppermute | solution.py:16
  239.1 7.5 %collective-permute-start.50 = (f32[2,34,1,256]{3,1,2,0:T(8,128)S(1)}, f32[2,34,1,256]{3,1,2,0:T(8,128)S(1)}, u32[]{:S(2)}, u32[]{:S(2)}) collective-permute-start(f32[2,34,1,256]{3,1,2,0:T(8,128)S(1)} %get-tuple-element.25), channel_id=1, source_target_pairs={{1,0},{2,1},{3,2},{4,3},{5,4},{6,5},{7,6},{9,8},{10,9},{11,10},{12... | collective-permute-start | bytes 208904 | tf_op jit(solution)/shard_map/ppermute | solution.py:17
  240.4 6.7 %collective-permute-start.51 = (f32[2,34,1,256]{3,1,2,0:T(8,128)S(1)}, f32[2,34,1,256]{3,1,2,0:T(8,128)S(1)}, u32[]{:S(2)}, u32[]{:S(2)}) collective-permute-start(f32[2,34,1,256]{3,1,2,0:T(8,128)S(1)} %get-tuple-element.26), channel_id=1, source_target_pairs={{0,1},{1,2},{2,3},{3,4},{4,5},{5,6},{6,7},{8,9},{9,10},{10,11},{11... | collective-permute-start | bytes 208904 | tf_op jit(solution)/shard_map/ppermute | solution.py:16
  439.6 30.3 %all-to-all-start.1 = ((f32[8,8,32,256]{3,2,1,0:T(8,128)}), f32[8,8,32,256]{3,2,1,0:T(8,128)S(1)}, u32[]{:S(2)}, u32[]{:S(2)}) async-start(f32[8,8,32,256]{3,2,1,0:T(8,128)} %copy.62), calls=%async_computation.1 | async-start | bytes 4194304 | tf_op jit(solution)/shard_map/all_to_all | solution.py:105
  (10 other events, 68.4 us)
where the time goes:
time: 481 us; the launch traced here: 472 us
  blocking collectives  152 us (32%)
  starting transfers between devices  147 us (31%)
  waiting for transfers between devices  66.8 us (14%)
  other arithmetic  53 us (11%)
  local copies, waits for them, and re-layouts  31.4 us (7%)
  matrix products  18.7 us (4%)
    ppermute x26, starting transfers between devices, extended(): before = lax.ppermute(last, axis, up)  109 us
    all_to_all x1, blocking collectives, shards(): lax.all_to_all(both, 'probe', split_axis=2, concat_axis=0, tiled=True)  79.6 us
    psum x1, blocking collectives, shards(): lax.psum(jnp.stack([partial_gram, partial_cross]), ('probe', 'sx', 'sy'))  72.6 us
    ppermute x26, starting transfers between devices, extended(): after = lax.ppermute(leading, axis, down)  34.3 us
    all_to_all x1, waiting for transfers between devices, shards(): lax.all_to_all(basis_slab.reshape(slabs[:, 0].shape), 'probe', split_axis...  25.3 us
    ppermute x26, waiting for transfers between devices, extended(): after = lax.ppermute(leading, axis, down)  24.1 us
    add x6, other arithmetic, forward_step(): result + (spread - 0.5 * cc[3]) * padded[..., 2:]  20.5 us
    ppermute x26, waiting for transfers between devices, extended(): before = lax.ppermute(last, axis, up)  17.3 us
  transfers between devices with their start and end apart: 53, of which 21 were waited for; matrix products, arithmetic and copies ran while one was open for 5% of the time, Pallas kernels for 0%

commit v1 on v0

--- a/solution.py
+++ b/solution.py
@@ -98,7 +98,9 @@
     flat_root = slabs[:, 1].reshape(count, -1)
     partial_gram = jnp.dot(flat, flat.T, precision=highest)
     partial_cross = jnp.dot(flat_root, flat_root.T, precision=highest)
-    sums = lax.psum(jnp.stack([partial_gram, partial_cross]), ("probe", "sx", "sy")) / ncells
+    sums = (
+        lax.psum(lax.psum(jnp.stack([partial_gram, partial_cross]), "probe"), ("sx", "sy")) / ncells
+    )
     gram, cross = (sums[0], sums[1])
     inverse = factor_inverse(gram, count)
     basis_slab = jnp.dot(inverse, flat, precision=highest)

time: 481 us -> 507 us (1.054)
  starting transfers between devices: 147 us -> 163 us
  blocking collectives: 152 us -> 163 us
    all_to_all x1, starting transfers between devices: 4.14 us -> 19.3 us  [shards(): lax.all_to_all(basis_slab.reshape(slabs[:, 0].shape), 'probe', split_axis...]
    psum x1 -> x2, blocking collectives: 72.6 us -> 83.7 us  [the longest x1 76 us: shards(): lax.psum(lax.psum(jnp.stack([partial_gram, partial_cross]), 'probe'), ('s...]
where the time goes in v1:
time: 507 us; the launch traced here: 498 us
  starting transfers between devices  163 us (32%)
  blocking collectives  163 us (32%)
  waiting for transfers between devices  66.8 us (13%)
  other arithmetic  53 us (10%)
  local copies, waits for them, and re-layouts  31.4 us (6%)
  matrix products  18.7 us (4%)
    ppermute x26, starting transfers between devices, extended(): before = lax.ppermute(last, axis, up)  109 us
    all_to_all x1, blocking collectives, shards(): lax.all_to_all(both, 'probe', split_axis=2, concat_axis=0, tiled=True)  79.6 us
    psum x1, blocking collectives, shards(): lax.psum(lax.psum(jnp.stack([partial_gram, partial_cross]), 'probe'), ('s...  76 us
    ppermute x26, starting transfers between devices, extended(): after = lax.ppermute(leading, axis, down)  34.3 us
    all_to_all x1, waiting for transfers between devices, shards(): lax.all_to_all(basis_slab.reshape(slabs[:, 0].shape), 'probe', split_axis...  25.3 us
    ppermute x26, waiting for transfers between devices, extended(): after = lax.ppermute(leading, axis, down)  24.1 us
    add x6, other arithmetic, forward_step(): result + (spread - 0.5 * cc[3]) * padded[..., 2:]  20.5 us
    all_to_all x1, starting transfers between devices, shards(): lax.all_to_all(basis_slab.reshape(slabs[:, 0].shape), 'probe', split_axis...  19.3 us
  transfers between devices with their start and end apart: 53, of which 21 were waited for; matrix products, arithmetic and copies ran while one was open for 5% of the time, Pallas kernels for 0%

profile of v1, /device:TPU:1, one launch (start us, length us, event | category | flops | bytes accessed | tf_op | source)
XLA Modules:
  0.0 497.9 jit_solution(16279369613025425369)
XLA Ops:
  3.0 4.6 collective-permute-start.1
  12.0 4.4 collective-permute-start.3
  21.8 3.5 fusion.10
  26.7 4.0 collective-permute-start.5
  33.3 4.9 collective-permute-start.7
  38.3 4.0 collective-permute-start.16
  43.6 3.5 fusion.14
  48.4 4.6 collective-permute-start.9
  53.3 4.4 collective-permute-start.18
  60.4 4.8 collective-permute-start.11
  68.3 3.4 fusion.18
  73.1 4.3 collective-permute-start.13
  80.0 4.4 collective-permute-start.15
  85.9 3.5 broadcast_multiply_fusion.3
  89.6 3.7 collective-permute-start.20
  98.3 4.3 collective-permute-start.22
  105.5 3.5 collective-permute-done.23
  109.5 3.9 broadcast_multiply_fusion.2
  113.5 3.5 collective-permute-start.24
  118.4 3.7 collective-permute-done.25
  122.1 4.3 collective-permute-start.26
  132.0 3.9 broadcast_multiply_fusion.1
  140.7 3.9 collective-permute-done.29
  149.4 3.5 collective-permute-done.31
  153.3 3.7 broadcast_multiply_fusion
  161.4 3.7 collective-permute-done.33
  165.1 4.3 collective-permute-start.34
  171.1 3.4 collective-permute-done.35
  179.1 4.0 collective-permute-start.37
  185.8 4.0 collective-permute-start.39
  192.0 3.4 fusion.27
  196.8 4.0 collective-permute-start.41
  203.5 4.4 collective-permute-start.43
  210.5 3.4 fusion.31
  215.3 4.4 collective-permute-start.45
  222.4 4.4 collective-permute-start.47
  233.2 4.6 collective-permute-start.49
  240.4 5.3 %collective-permute-start.51 = (f32[2,34,1,256]{3,1,2,0:T(8,128)S(1)}, f32[2,34,1,256]{3,1,2,0:T(8,128)S(1)}, u32[]{:S(2)}, u32[]{:S(2)}) collective-permute-start(f32[2,34,1,256]{3,1,2,0:T(8,128)S(1)} %get-tuple-element.26), channel_id=1, source_target_pairs={{0,1},{1,2},{2,3},{3,4},{4,5},{5,6},{6,7},{8,9},{9,10},{10,11},{11... | collective-permute-start | bytes 208904 | tf_op jit(solution)/shard_map/ppermute | solution.py:16
  247.1 3.5 fusion.41
  253.3 79.6 %all_to_all.36 = f32[2,2,32,32,256]{4,3,0,1,2:T(8,128)S(1)} all-to-all(f32[2,2,32,32,256]{4,3,0,1,2:T(8,128)S(1)} %copy.58), channel_id=1, replica_groups=mesh['probe'=4,'sx'=4,'sy'=8] {'probe'}, dimensions={2} | all-to-all | bytes 8388608 | tf_op jit(solution)/shard_map/all_to_all | solution.py:96
  333.0 5.2 %copy.72 = f32[2,2,4,8,32,256]{5,0,2,4,3,1:T(2,128)} copy(f32[2,2,4,8,32,256]{5,4,0,1,3,2:T(8,128)S(1)} %bitcast.90) | data formatting | bytes 8388608 | tf_op jit(solution)/shard_map/all_to_all | solution.py:96
  338.2 6.1 %all_to_all.29 = f32[8,2,8,32,256]{4,0,3,2,1:T(8,128)} reshape(f32[4,2,2,8,32,256]{5,1,0,4,3,2:T(2,128)} %bitcast.91) | data formatting | bytes 8388608 | tf_op jit(solution)/shard_map/all_to_all | solution.py:96
  344.4 7.1 %fusion.131 = f32[1,8,8]{2,1,0:T(8,128)S(1)} fusion(f32[8,2,8,32,256]{4,0,3,2,1:T(8,128)} %all_to_all.29), kind=kOutput, calls=%fused_computation.253 | convolution fusion | flops 50331648 | bytes 2097408 | tf_op jit(solution)/shard_map/dot_general | solution.py:99
  351.5 7.1 %fusion.134 = f32[1,8,8]{2,1,0:T(8,128)S(1)} fusion(f32[8,2,8,32,256]{4,0,3,2,1:T(8,128)} %all_to_all.29), kind=kOutput, calls=%fused_computation.254 | convolution fusion | flops 50331648 | bytes 2097408 | tf_op jit(solution)/shard_map/dot_general | solution.py:100
  358.6 7.6 %psum.14 = f32[2,8,8]{2,1,0:T(8,128)S(1)} all-reduce(f32[2,8,8]{2,1,0:T(8,128)S(1)} %pad_maximum_fusion.117), channel_id=1, replica_groups=mesh['probe'=4,'sx'=4,'sy'=8] {'probe'}, use_global_device_ids=true, to_apply=%region_0.1 | all-reduce | flops 128 | bytes 1024 | tf_op jit(solution)/shard_map/psum | solution.py:102
  366.2 76.0 %psum.15 = f32[2,8,8]{2,1,0:T(8,128)S(1)} all-reduce(f32[2,8,8]{2,1,0:T(8,128)S(1)} %psum.14), channel_id=1, replica_groups=mesh['probe'=4,'sx'=4,'sy'=8] {'sx','sy'}, use_global_device_ids=true, to_apply=%region_1.2 | all-reduce | flops 128 | bytes 1024 | tf_op jit(solution)/shard_map/psum | solution.py:102
  450.6 19.3 %all-to-all-start.1 = ((f32[8,8,32,256]{3,2,1,0:T(8,128)}), f32[8,8,32,256]{3,2,1,0:T(8,128)S(1)}, u32[]{:S(2)}, u32[]{:S(2)}) async-start(f32[8,8,32,256]{3,2,1,0:T(8,128)} %copy.62), calls=%async_computation.1 | async-start | bytes 4194304 | tf_op jit(solution)/shard_map/all_to_all | solution.py:107
  470.8 25.3 %all-to-all-done.1 = f32[8,8,32,256]{3,2,1,0:T(8,128)S(1)} async-done(((f32[8,8,32,256]{3,2,1,0:T(8,128)}), f32[8,8,32,256]{3,2,1,0:T(8,128)S(1)}, u32[]{:S(2)}, u32[]{:S(2)}) %all-to-all-start.1) | async-done | bytes 2097184 | tf_op jit(solution)/shard_map/all_to_all | solution.py:107
  (168 shorter events, 105.2 us)
Async XLA Ops:
  1.6 8.9 %collective-permute-start = (f32[2,1,32,256]{3,1,2,0:T(1,128)S(1)}, f32[2,1,32,256]{3,1,2,0:T(1,128)S(1)}, u32[]{:S(2)}, u32[]{:S(2)}) collective-permute-start(f32[2,1,32,256]{3,1,2,0:T(1,128)S(1)} %copy.38), channel_id=1, source_target_pairs={{8,0},{16,8},{24,16},{9,1},{17,9},{25,17},{10,2},{18,10},{26,18},{... | collective-permute-start | bytes 196616 | tf_op jit(solution)/shard_map/ppermute | solution.py:17
  3.0 7.6 %collective-permute-start.1 = (f32[2,1,32,256]{3,1,2,0:T(1,128)S(1)}, f32[2,1,32,256]{3,1,2,0:T(1,128)S(1)}, u32[]{:S(2)}, u32[]{:S(2)}) collective-permute-start(f32[2,1,32,256]{3,1,2,0:T(1,128)S(1)} %copy.41), channel_id=1, source_target_pairs={{0,8},{8,16},{16,24},{1,9},{9,17},{17,25},{2,10},{10,18},{18,26},{... | collective-permute-start | bytes 196616 | tf_op jit(solution)/shard_map/ppermute | solution.py:16
  10.6 11.2 %collective-permute-start.2 = (f32[2,34,1,256]{3,1,2,0:T(8,128)S(1)}, f32[2,34,1,256]{3,1,2,0:T(8,128)S(1)}, u32[]{:S(2)}, u32[]{:S(2)}) collective-permute-start(f32[2,34,1,256]{3,1,2,0:T(8,128)S(1)} %get-tuple-element.47), channel_id=1, source_target_pairs={{1,0},{2,1},{3,2},{4,3},{5,4},{6,5},{7,6},{9,8},{10,9},{11,10},{12... | collective-permute-start | bytes 208904 | tf_op jit(solution)/shard_map/ppermute | solution.py:17
  12.0 9.8 %collective-permute-start.3 = (f32[2,34,1,256]{3,1,2,0:T(8,128)S(1)}, f32[2,34,1,256]{3,1,2,0:T(8,128)S(1)}, u32[]{:S(2)}, u32[]{:S(2)}) collective-permute-start(f32[2,34,1,256]{3,1,2,0:T(8,128)S(1)} %get-tuple-element.48), channel_id=1, source_target_pairs={{0,1},{1,2},{2,3},{3,4},{4,5},{5,6},{6,7},{8,9},{9,10},{10,11},{11... | collective-permute-start | bytes 208904 | tf_op jit(solution)/shard_map/ppermute | solution.py:16
  25.4 5.3 %collective-permute-start.4 = (f32[2,1,32,256]{3,1,2,0:T(1,128)S(1)}, f32[2,1,32,256]{3,1,2,0:T(1,128)S(1)}, u32[]{:S(2)}, u32[]{:S(2)}) collective-permute-start(f32[2,1,32,256]{3,1,2,0:T(1,128)S(1)} %get-tuple-element.70), channel_id=1, source_target_pairs={{8,0},{16,8},{24,16},{9,1},{17,9},{25,17},{10,2},{18,10},{26,18},{... | collective-permute-start | bytes 196616 | tf_op jit(solution)/shard_map/ppermute | solution.py:17
  26.7 5.3 %collective-permute-start.5 = (f32[2,1,32,256]{3,1,2,0:T(1,128)S(1)}, f32[2,1,32,256]{3,1,2,0:T(1,128)S(1)}, u32[]{:S(2)}, u32[]{:S(2)}) collective-permute-start(f32[2,1,32,256]{3,1,2,0:T(1,128)S(1)} %get-tuple-element.69), channel_id=1, source_target_pairs={{0,8},{8,16},{16,24},{1,9},{9,17},{17,25},{2,10},{10,18},{18,26},{... | collective-permute-start | bytes 196616 | tf_op jit(solution)/shard_map/ppermute | solution.py:16
  32.0 11.5 %collective-permute-start.6 = (f32[2,34,1,256]{3,1,2,0:T(8,128)S(1)}, f32[2,34,1,256]{3,1,2,0:T(8,128)S(1)}, u32[]{:S(2)}, u32[]{:S(2)}) collective-permute-start(f32[2,34,1,256]{3,1,2,0:T(8,128)S(1)} %get-tuple-element.45), channel_id=1, source_target_pairs={{1,0},{2,1},{3,2},{4,3},{5,4},{6,5},{7,6},{9,8},{10,9},{11,10},{12... | collective-permute-start | bytes 208904 | tf_op jit(solution)/shard_map/ppermute | solution.py:17
  33.3 10.2 %collective-permute-start.7 = (f32[2,34,1,256]{3,1,2,0:T(8,128)S(1)}, f32[2,34,1,256]{3,1,2,0:T(8,128)S(1)}, u32[]{:S(2)}, u32[]{:S(2)}) collective-permute-start(f32[2,34,1,256]{3,1,2,0:T(8,128)S(1)} %get-tuple-element.46), channel_id=1, source_target_pairs={{0,1},{1,2},{2,3},{3,4},{4,5},{5,6},{6,7},{8,9},{9,10},{10,11},{11... | collective-permute-start | bytes 208904 | tf_op jit(solution)/shard_map/ppermute | solution.py:16
  38.3 14.8 %collective-permute-start.16 = (f32[4,1,32,256]{3,2,1,0:T(8,128)S(1)}, f32[4,1,32,256]{3,2,1,0:T(8,128)S(1)}, u32[]{:S(2)}, u32[]{:S(2)}) collective-permute-start(f32[4,1,32,256]{3,2,1,0:T(8,128)S(1)} %get-tuple-element.17), channel_id=1, source_target_pairs={{0,8},{8,16},{16,24},{1,9},{9,17},{17,25},{2,10},{10,18},{18,26},{... | collective-permute-start | bytes 393224 | tf_op jit(solution)/shard_map/ppermute | solution.py:16
  42.3 10.8 %collective-permute-start.17 = (f32[4,1,32,256]{3,2,1,0:T(8,128)S(1)}, f32[4,1,32,256]{3,2,1,0:T(8,128)S(1)}, u32[]{:S(2)}, u32[]{:S(2)}) collective-permute-start(f32[4,1,32,256]{3,2,1,0:T(8,128)S(1)} %get-tuple-element.18), channel_id=1, source_target_pairs={{8,0},{16,8},{24,16},{9,1},{17,9},{25,17},{10,2},{18,10},{26,18},{... | collective-permute-start | bytes 393224 | tf_op jit(solution)/shard_map/ppermute | solution.py:17
  47.1 11.9 %collective-permute-start.8 = (f32[2,1,32,256]{3,1,2,0:T(1,128)S(1)}, f32[2,1,32,256]{3,1,2,0:T(1,128)S(1)}, u32[]{:S(2)}, u32[]{:S(2)}) collective-permute-start(f32[2,1,32,256]{3,1,2,0:T(1,128)S(1)} %get-tuple-element.68), channel_id=1, source_target_pairs={{8,0},{16,8},{24,16},{9,1},{17,9},{25,17},{10,2},{18,10},{26,18},{... | collective-permute-start | bytes 196616 | tf_op jit(solution)/shard_map/ppermute | solution.py:17
  48.4 10.6 %collective-permute-start.9 = (f32[2,1,32,256]{3,1,2,0:T(1,128)S(1)}, f32[2,1,32,256]{3,1,2,0:T(1,128)S(1)}, u32[]{:S(2)}, u32[]{:S(2)}) collective-permute-start(f32[2,1,32,256]{3,1,2,0:T(1,128)S(1)} %get-tuple-element.67), channel_id=1, source_target_pairs={{0,8},{8,16},{16,24},{1,9},{9,17},{17,25},{2,10},{10,18},{18,26},{... | collective-permute-start | bytes 196616 | tf_op jit(solution)/shard_map/ppermute | solution.py:16
  53.3 12.5 %collective-permute-start.18 = (f32[4,34,1,256]{3,1,2,0:T(8,128)S(1)}, f32[4,34,1,256]{3,1,2,0:T(8,128)S(1)}, u32[]{:S(2)}, u32[]{:S(2)}) collective-permute-start(f32[4,34,1,256]{3,1,2,0:T(8,128)S(1)} %copy.49), channel_id=1, source_target_pairs={{0,1},{1,2},{2,3},{3,4},{4,5},{5,6},{6,7},{8,9},{9,10},{10,11},{11... | collective-permute-start | bytes 417800 | tf_op jit(solution)/shard_map/ppermute | solution.py:16
  57.8 8.2 %collective-permute-start.19 = (f32[4,34,1,256]{3,1,2,0:T(8,128)S(1)}, f32[4,34,1,256]{3,1,2,0:T(8,128)S(1)}, u32[]{:S(2)}, u32[]{:S(2)}) collective-permute-start(f32[4,34,1,256]{3,1,2,0:T(8,128)S(1)} %copy.50), channel_id=1, source_target_pairs={{1,0},{2,1},{3,2},{4,3},{5,4},{6,5},{7,6},{9,8},{10,9},{11,10},{12... | collective-permute-start | bytes 417800 | tf_op jit(solution)/shard_map/ppermute | solution.py:17
  59.1 7.1 %collective-permute-start.10 = (f32[2,34,1,256]{3,1,2,0:T(8,128)S(1)}, f32[2,34,1,256]{3,1,2,0:T(8,128)S(1)}, u32[]{:S(2)}, u32[]{:S(2)}) collective-permute-start(f32[2,34,1,256]{3,1,2,0:T(8,128)S(1)} %get-tuple-element.43), channel_id=1, source_target_pairs={{1,0},{2,1},{3,2},{4,3},{5,4},{6,5},{7,6},{9,8},{10,9},{11,10},{12... | collective-permute-start | bytes 208904 | tf_op jit(solution)/shard_map/ppermute | solution.py:17
  60.4 7.9 %collective-permute-start.11 = (f32[2,34,1,256]{3,1,2,0:T(8,128)S(1)}, f32[2,34,1,256]{3,1,2,0:T(8,128)S(1)}, u32[]{:S(2)}, u32[]{:S(2)}) collective-permute-start(f32[2,34,1,256]{3,1,2,0:T(8,128)S(1)} %get-tuple-element.44), channel_id=1, source_target_pairs={{0,1},{1,2},{2,3},{3,4},{4,5},{5,6},{6,7},{8,9},{9,10},{10,11},{11... | collective-permute-start | bytes 208904 | tf_op jit(solution)/shard_map/ppermute | solution.py:16
  71.8 6.1 %collective-permute-start.12 = (f32[2,1,32,256]{3,1,2,0:T(1,128)S(1)}, f32[2,1,32,256]{3,1,2,0:T(1,128)S(1)}, u32[]{:S(2)}, u32[]{:S(2)}) collective-permute-start(f32[2,1,32,256]{3,1,2,0:T(1,128)S(1)} %get-tuple-element.66), channel_id=1, source_target_pairs={{8,0},{16,8},{24,16},{9,1},{17,9},{25,17},{10,2},{18,10},{26,18},{... | collective-permute-start | bytes 196616 | tf_op jit(solution)/shard_map/ppermute | solution.py:17
  73.1 5.6 %collective-permute-start.13 = (f32[2,1,32,256]{3,1,2,0:T(1,128)S(1)}, f32[2,1,32,256]{3,1,2,0:T(1,128)S(1)}, u32[]{:S(2)}, u32[]{:S(2)}) collective-permute-start(f32[2,1,32,256]{3,1,2,0:T(1,128)S(1)} %get-tuple-element.65), channel_id=1, source_target_pairs={{0,8},{8,16},{16,24},{1,9},{9,17},{17,25},{2,10},{10,18},{18,26},{... | collective-permute-start | bytes 196616 | tf_op jit(solution)/shard_map/ppermute | solution.py:16
  78.7 6.1 %collective-permute-start.14 = (f32[2,34,1,256]{3,1,2,0:T(8,128)S(1)}, f32[2,34,1,256]{3,1,2,0:T(8,128)S(1)}, u32[]{:S(2)}, u32[]{:S(2)}) collective-permute-start(f32[2,34,1,256]{3,1,2,0:T(8,128)S(1)} %get-tuple-element.41), channel_id=1, source_target_pairs={{1,0},{2,1},{3,2},{4,3},{5,4},{6,5},{7,6},{9,8},{10,9},{11,10},{12... | collective-permute-start | bytes 208904 | tf_op jit(solution)/shard_map/ppermute | solution.py:17
  80.0 5.9 %collective-permute-start.15 = (f32[2,34,1,256]{3,1,2,0:T(8,128)S(1)}, f32[2,34,1,256]{3,1,2,0:T(8,128)S(1)}, u32[]{:S(2)}, u32[]{:S(2)}) collective-permute-start(f32[2,34,1,256]{3,1,2,0:T(8,128)S(1)} %get-tuple-element.42), channel_id=1, source_target_pairs={{0,1},{1,2},{2,3},{3,4},{4,5},{5,6},{6,7},{8,9},{9,10},{10,11},{11... | collective-permute-start | bytes 208904 | tf_op jit(solution)/shard_map/ppermute | solution.py:16
  89.6 8.2 %collective-permute-start.20 = (f32[2,1,32,256]{3,1,2,0:T(1,128)S(1)}, f32[2,1,32,256]{3,1,2,0:T(1,128)S(1)}, u32[]{:S(2)}, u32[]{:S(2)}) collective-permute-start(f32[2,1,32,256]{3,1,2,0:T(1,128)S(1)} %get-tuple-element.63), channel_id=1, source_target_pairs={{0,8},{8,16},{16,24},{1,9},{9,17},{17,25},{2,10},{10,18},{18,26},{... | collective-permute-start | bytes 196616 | tf_op jit(solution)/shard_map/ppermute | solution.py:16
  93.3 5.0 %collective-permute-start.21 = (f32[2,1,32,256]{3,1,2,0:T(1,128)S(1)}, f32[2,1,32,256]{3,1,2,0:T(1,128)S(1)}, u32[]{:S(2)}, u32[]{:S(2)}) collective-permute-start(f32[2,1,32,256]{3,1,2,0:T(1,128)S(1)} %get-tuple-element.64), channel_id=1, source_target_pairs={{8,0},{16,8},{24,16},{9,1},{17,9},{25,17},{10,2},{18,10},{26,18},{... | collective-permute-start | bytes 196616 | tf_op jit(solution)/shard_map/ppermute | solution.py:17
  98.3 7.2 %collective-permute-start.22 = (f32[2,34,1,256]{3,1,2,0:T(8,128)S(1)}, f32[2,34,1,256]{3,1,2,0:T(8,128)S(1)}, u32[]{:S(2)}, u32[]{:S(2)}) collective-permute-start(f32[2,34,1,256]{3,1,2,0:T(8,128)S(1)} %get-tuple-element.39), channel_id=1, source_target_pairs={{0,1},{1,2},{2,3},{3,4},{4,5},{5,6},{6,7},{8,9},{9,10},{10,11},{11... | collective-permute-start | bytes 208904 | tf_op jit(solution)/shard_map/ppermute | solution.py:16
  102.6 6.4 %collective-permute-start.23 = (f32[2,34,1,256]{3,1,2,0:T(8,128)S(1)}, f32[2,34,1,256]{3,1,2,0:T(8,128)S(1)}, u32[]{:S(2)}, u32[]{:S(2)}) collective-permute-start(f32[2,34,1,256]{3,1,2,0:T(8,128)S(1)} %get-tuple-element.40), channel_id=1, source_target_pairs={{1,0},{2,1},{3,2},{4,3},{5,4},{6,5},{7,6},{9,8},{10,9},{11,10},{12... | collective-permute-start | bytes 208904 | tf_op jit(solution)/shard_map/ppermute | solution.py:17
  117.0 5.0 %collective-permute-start.25 = (f32[2,1,32,256]{3,1,2,0:T(1,128)S(1)}, f32[2,1,32,256]{3,1,2,0:T(1,128)S(1)}, u32[]{:S(2)}, u32[]{:S(2)}) collective-permute-start(f32[2,1,32,256]{3,1,2,0:T(1,128)S(1)} %get-tuple-element.62), channel_id=1, source_target_pairs={{8,0},{16,8},{24,16},{9,1},{17,9},{25,17},{10,2},{18,10},{26,18},{... | collective-permute-start | bytes 196616 | tf_op jit(solution)/shard_map/ppermute | solution.py:17
  122.1 7.6 %collective-permute-start.26 = (f32[2,34,1,256]{3,1,2,0:T(8,128)S(1)}, f32[2,34,1,256]{3,1,2,0:T(8,128)S(1)}, u32[]{:S(2)}, u32[]{:S(2)}) collective-permute-start(f32[2,34,1,256]{3,1,2,0:T(8,128)S(1)} %get-tuple-element.37), channel_id=1, source_target_pairs={{0,1},{1,2},{2,3},{3,4},{4,5},{5,6},{6,7},{8,9},{9,10},{10,11},{11... | collective-permute-start | bytes 208904 | tf_op jit(solution)/shard_map/ppermute | solution.py:16
  126.3 5.2 %collective-permute-start.27 = (f32[2,34,1,256]{3,1,2,0:T(8,128)S(1)}, f32[2,34,1,256]{3,1,2,0:T(8,128)S(1)}, u32[]{:S(2)}, u32[]{:S(2)}) collective-permute-start(f32[2,34,1,256]{3,1,2,0:T(8,128)S(1)} %get-tuple-element.38), channel_id=1, source_target_pairs={{1,0},{2,1},{3,2},{4,3},{5,4},{6,5},{7,6},{9,8},{10,9},{11,10},{12... | collective-permute-start | bytes 208904 | tf_op jit(solution)/shard_map/ppermute | solution.py:17
  139.4 5.2 %collective-permute-start.29 = (f32[2,1,32,256]{3,1,2,0:T(1,128)S(1)}, f32[2,1,32,256]{3,1,2,0:T(1,128)S(1)}, u32[]{:S(2)}, u32[]{:S(2)}) collective-permute-start(f32[2,1,32,256]{3,1,2,0:T(1,128)S(1)} %get-tuple-element.60), channel_id=1, source_target_pairs={{8,0},{16,8},{24,16},{9,1},{17,9},{25,17},{10,2},{18,10},{26,18},{... | collective-permute-start | bytes 196616 | tf_op jit(solution)/shard_map/ppermute | solution.py:17
  147.7 5.2 %collective-permute-start.31 = (f32[2,34,1,256]{3,1,2,0:T(8,128)S(1)}, f32[2,34,1,256]{3,1,2,0:T(8,128)S(1)}, u32[]{:S(2)}, u32[]{:S(2)}) collective-permute-start(f32[2,34,1,256]{3,1,2,0:T(8,128)S(1)} %get-tuple-element.36), channel_id=1, source_target_pairs={{1,0},{2,1},{3,2},{4,3},{5,4},{6,5},{7,6},{9,8},{10,9},{11,10},{12... | collective-permute-start | bytes 208904 | tf_op jit(solution)/shard_map/ppermute | solution.py:17
  165.1 6.0 %collective-permute-start.34 = (f32[2,34,1,256]{3,1,2,0:T(8,128)S(1)}, f32[2,34,1,256]{3,1,2,0:T(8,128)S(1)}, u32[]{:S(2)}, u32[]{:S(2)}) collective-permute-start(f32[2,34,1,256]{3,1,2,0:T(8,128)S(1)} %get-tuple-element.33), channel_id=1, source_target_pairs={{0,1},{1,2},{2,3},{3,4},{4,5},{5,6},{6,7},{8,9},{9,10},{10,11},{11... | collective-permute-start | bytes 208904 | tf_op jit(solution)/shard_map/ppermute | solution.py:16
  169.4 5.2 %collective-permute-start.35 = (f32[2,34,1,256]{3,1,2,0:T(8,128)S(1)}, f32[2,34,1,256]{3,1,2,0:T(8,128)S(1)}, u32[]{:S(2)}, u32[]{:S(2)}) collective-permute-start(f32[2,34,1,256]{3,1,2,0:T(8,128)S(1)} %get-tuple-element.34), channel_id=1, source_target_pairs={{1,0},{2,1},{3,2},{4,3},{5,4},{6,5},{7,6},{9,8},{10,9},{11,10},{12... | collective-permute-start | bytes 208904 | tf_op jit(solution)/shard_map/ppermute | solution.py:17
  177.8 5.3 %collective-permute-start.36 = (f32[2,1,32,256]{3,1,2,0:T(1,128)S(1)}, f32[2,1,32,256]{3,1,2,0:T(1,128)S(1)}, u32[]{:S(2)}, u32[]{:S(2)}) collective-permute-start(f32[2,1,32,256]{3,1,2,0:T(1,128)S(1)} %get-tuple-element.56), channel_id=1, source_target_pairs={{8,0},{16,8},{24,16},{9,1},{17,9},{25,17},{10,2},{18,10},{26,18},{... | collective-permute-start | bytes 196616 | tf_op jit(solution)/shard_map/ppermute | solution.py:17
  179.1 5.3 %collective-permute-start.37 = (f32[2,1,32,256]{3,1,2,0:T(1,128)S(1)}, f32[2,1,32,256]{3,1,2,0:T(1,128)S(1)}, u32[]{:S(2)}, u32[]{:S(2)}) collective-permute-start(f32[2,1,32,256]{3,1,2,0:T(1,128)S(1)} %get-tuple-element.55), channel_id=1, source_target_pairs={{0,8},{8,16},{16,24},{1,9},{9,17},{17,25},{2,10},{10,18},{18,26},{... | collective-permute-start | bytes 196616 | tf_op jit(solution)/shard_map/ppermute | solution.py:16
  184.5 5.3 %collective-permute-start.38 = (f32[2,34,1,256]{3,1,2,0:T(8,128)S(1)}, f32[2,34,1,256]{3,1,2,0:T(8,128)S(1)}, u32[]{:S(2)}, u32[]{:S(2)}) collective-permute-start(f32[2,34,1,256]{3,1,2,0:T(8,128)S(1)} %get-tuple-element.31), channel_id=1, source_target_pairs={{1,0},{2,1},{3,2},{4,3},{5,4},{6,5},{7,6},{9,8},{10,9},{11,10},{12... | collective-permute-start | bytes 208904 | tf_op jit(solution)/shard_map/ppermute | solution.py:17
  185.8 6.2 %collective-permute-start.39 = (f32[2,34,1,256]{3,1,2,0:T(8,128)S(1)}, f32[2,34,1,256]{3,1,2,0:T(8,128)S(1)}, u32[]{:S(2)}, u32[]{:S(2)}) collective-permute-start(f32[2,34,1,256]{3,1,2,0:T(8,128)S(1)} %get-tuple-element.32), channel_id=1, source_target_pairs={{0,1},{1,2},{2,3},{3,4},{4,5},{5,6},{6,7},{8,9},{9,10},{10,11},{11... | collective-permute-start | bytes 208904 | tf_op jit(solution)/shard_map/ppermute | solution.py:16
  195.5 5.3 %collective-permute-start.40 = (f32[2,1,32,256]{3,1,2,0:T(1,128)S(1)}, f32[2,1,32,256]{3,1,2,0:T(1,128)S(1)}, u32[]{:S(2)}, u32[]{:S(2)}) collective-permute-start(f32[2,1,32,256]{3,1,2,0:T(1,128)S(1)} %get-tuple-element.54), channel_id=1, source_target_pairs={{8,0},{16,8},{24,16},{9,1},{17,9},{25,17},{10,2},{18,10},{26,18},{... | collective-permute-start | bytes 196616 | tf_op jit(solution)/shard_map/ppermute | solution.py:17
  196.8 5.3 %collective-permute-start.41 = (f32[2,1,32,256]{3,1,2,0:T(1,128)S(1)}, f32[2,1,32,256]{3,1,2,0:T(1,128)S(1)}, u32[]{:S(2)}, u32[]{:S(2)}) collective-permute-start(f32[2,1,32,256]{3,1,2,0:T(1,128)S(1)} %get-tuple-element.53), channel_id=1, source_target_pairs={{0,8},{8,16},{16,24},{1,9},{9,17},{17,25},{2,10},{10,18},{18,26},{... | collective-permute-start | bytes 196616 | tf_op jit(solution)/shard_map/ppermute | solution.py:16
  202.2 5.8 %collective-permute-start.42 = (f32[2,34,1,256]{3,1,2,0:T(8,128)S(1)}, f32[2,34,1,256]{3,1,2,0:T(8,128)S(1)}, u32[]{:S(2)}, u32[]{:S(2)}) collective-permute-start(f32[2,34,1,256]{3,1,2,0:T(8,128)S(1)} %get-tuple-element.29), channel_id=1, source_target_pairs={{1,0},{2,1},{3,2},{4,3},{5,4},{6,5},{7,6},{9,8},{10,9},{11,10},{12... | collective-permute-start | bytes 208904 | tf_op jit(solution)/shard_map/ppermute | solution.py:17
  203.5 7.0 %collective-permute-start.43 = (f32[2,34,1,256]{3,1,2,0:T(8,128)S(1)}, f32[2,34,1,256]{3,1,2,0:T(8,128)S(1)}, u32[]{:S(2)}, u32[]{:S(2)}) collective-permute-start(f32[2,34,1,256]{3,1,2,0:T(8,128)S(1)} %get-tuple-element.30), channel_id=1, source_target_pairs={{0,1},{1,2},{2,3},{3,4},{4,5},{5,6},{6,7},{8,9},{9,10},{10,11},{11... | collective-permute-start | bytes 208904 | tf_op jit(solution)/shard_map/ppermute | solution.py:16
  214.0 5.8 %collective-permute-start.44 = (f32[2,1,32,256]{3,1,2,0:T(1,128)S(1)}, f32[2,1,32,256]{3,1,2,0:T(1,128)S(1)}, u32[]{:S(2)}, u32[]{:S(2)}) collective-permute-start(f32[2,1,32,256]{3,1,2,0:T(1,128)S(1)} %get-tuple-element.52), channel_id=1, source_target_pairs={{8,0},{16,8},{24,16},{9,1},{17,9},{25,17},{10,2},{18,10},{26,18},{... | collective-permute-start | bytes 196616 | tf_op jit(solution)/shard_map/ppermute | solution.py:17
  215.3 5.8 %collective-permute-start.45 = (f32[2,1,32,256]{3,1,2,0:T(1,128)S(1)}, f32[2,1,32,256]{3,1,2,0:T(1,128)S(1)}, u32[]{:S(2)}, u32[]{:S(2)}) collective-permute-start(f32[2,1,32,256]{3,1,2,0:T(1,128)S(1)} %get-tuple-element.51), channel_id=1, source_target_pairs={{0,8},{8,16},{16,24},{1,9},{9,17},{17,25},{2,10},{10,18},{18,26},{... | collective-permute-start | bytes 196616 | tf_op jit(solution)/shard_map/ppermute | solution.py:16
  221.1 5.8 %collective-permute-start.46 = (f32[2,34,1,256]{3,1,2,0:T(8,128)S(1)}, f32[2,34,1,256]{3,1,2,0:T(8,128)S(1)}, u32[]{:S(2)}, u32[]{:S(2)}) collective-permute-start(f32[2,34,1,256]{3,1,2,0:T(8,128)S(1)} %get-tuple-element.27), channel_id=1, source_target_pairs={{1,0},{2,1},{3,2},{4,3},{5,4},{6,5},{7,6},{9,8},{10,9},{11,10},{12... | collective-permute-start | bytes 208904 | tf_op jit(solution)/shard_map/ppermute | solution.py:17
  222.4 5.9 %collective-permute-start.47 = (f32[2,34,1,256]{3,1,2,0:T(8,128)S(1)}, f32[2,34,1,256]{3,1,2,0:T(8,128)S(1)}, u32[]{:S(2)}, u32[]{:S(2)}) collective-permute-start(f32[2,34,1,256]{3,1,2,0:T(8,128)S(1)} %get-tuple-element.28), channel_id=1, source_target_pairs={{0,1},{1,2},{2,3},{3,4},{4,5},{5,6},{6,7},{8,9},{9,10},{10,11},{11... | collective-permute-start | bytes 208904 | tf_op jit(solution)/shard_map/ppermute | solution.py:16
  231.7 6.1 %collective-permute-start.48 = (f32[2,1,32,256]{3,1,2,0:T(1,128)S(1)}, f32[2,1,32,256]{3,1,2,0:T(1,128)S(1)}, u32[]{:S(2)}, u32[]{:S(2)}) collective-permute-start(f32[2,1,32,256]{3,1,2,0:T(1,128)S(1)} %get-tuple-element.50), channel_id=1, source_target_pairs={{8,0},{16,8},{24,16},{9,1},{17,9},{25,17},{10,2},{18,10},{26,18},{... | collective-permute-start | bytes 196616 | tf_op jit(solution)/shard_map/ppermute | solution.py:17
  233.2 5.9 %collective-permute-start.49 = (f32[2,1,32,256]{3,1,2,0:T(1,128)S(1)}, f32[2,1,32,256]{3,1,2,0:T(1,128)S(1)}, u32[]{:S(2)}, u32[]{:S(2)}) collective-permute-start(f32[2,1,32,256]{3,1,2,0:T(1,128)S(1)} %get-tuple-element.49), channel_id=1, source_target_pairs={{0,8},{8,16},{16,24},{1,9},{9,17},{17,25},{2,10},{10,18},{18,26},{... | collective-permute-start | bytes 196616 | tf_op jit(solution)/shard_map/ppermute | solution.py:16
  239.1 7.5 %collective-permute-start.50 = (f32[2,34,1,256]{3,1,2,0:T(8,128)S(1)}, f32[2,34,1,256]{3,1,2,0:T(8,128)S(1)}, u32[]{:S(2)}, u32[]{:S(2)}) collective-permute-start(f32[2,34,1,256]{3,1,2,0:T(8,128)S(1)} %get-tuple-element.25), channel_id=1, source_target_pairs={{1,0},{2,1},{3,2},{4,3},{5,4},{6,5},{7,6},{9,8},{10,9},{11,10},{12... | collective-permute-start | bytes 208904 | tf_op jit(solution)/shard_map/ppermute | solution.py:17
  240.4 6.7 %collective-permute-start.51 = (f32[2,34,1,256]{3,1,2,0:T(8,128)S(1)}, f32[2,34,1,256]{3,1,2,0:T(8,128)S(1)}, u32[]{:S(2)}, u32[]{:S(2)}) collective-permute-start(f32[2,34,1,256]{3,1,2,0:T(8,128)S(1)} %get-tuple-element.26), channel_id=1, source_target_pairs={{0,1},{1,2},{2,3},{3,4},{4,5},{5,6},{6,7},{8,9},{9,10},{10,11},{11... | collective-permute-start | bytes 208904 | tf_op jit(solution)/shard_map/ppermute | solution.py:16
  450.6 45.5 %all-to-all-start.1 = ((f32[8,8,32,256]{3,2,1,0:T(8,128)}), f32[8,8,32,256]{3,2,1,0:T(8,128)S(1)}, u32[]{:S(2)}, u32[]{:S(2)}) async-start(f32[8,8,32,256]{3,2,1,0:T(8,128)} %copy.62), calls=%async_computation.1 | async-start | bytes 4194304 | tf_op jit(solution)/shard_map/all_to_all | solution.py:107
  (10 other events, 68.4 us)
